TPU v7x, 256 devices: a whole 4x4x8 slice. The times are simulated.
256 devices in a mesh: row: 8 (over z), col: 32 (over y, x, core).
Axes of the slice: x: 4, y: 4, z: 8, core: 2. Of those that a mesh axis runs over, the one named last changes fastest.
Arguments:
- ancestor_inverse: bfloat16 [24576, 24576], P('row', 'col'), may hold values from -6 to 6
- factor_slots: bfloat16 [3, 16384, 512], P(None, ('row', 'col')), may hold values from -0.25 to 0.25
- slot_tiles: int32 [3, 64], replicated, may hold values from -1 to 95, as said below
- parent_factor: bfloat16 [2, 512, 512], replicated, may hold values from -0.25 to 0.25
- diag_inverse: float32 [3, 512, 512], replicated, may hold values from -6 to 6
Outputs:
- inverse_panels: bfloat16 [3, 24576, 512], P(None, ('row', 'col'))
- diag_blocks: float32 [3, 512, 512], replicated
- parent_blocks: float32 [2, 512, 512], replicated
Inputs may be any that keep to these rules, and one draw needn't show every extreme that they name: `slot_tiles`: entries b * 2 to b * 2 + 1 of a supernode's row are the slots of column block b: each is -1 (empty) or names a tile from b * 3 to b * 3 + 2, no tile twice; in each supernode some block has all its slots filled. `factor_slots`: rows of an empty slot are not part of the factor.
All inputs are finite; a program needn't handle non-finite values.
Results may differ from a plain program's by a relative error of at most 0.00075.
Values may be sent and summed in bfloat16 or wider, within the bound.
No kernel may reach another device: no remote copies, remote signals or barrier semaphores. Data moves between devices by JAX's collectives and lax.ppermute only.
A program may use at most 128 MiB of HBM per device.

v0:
```python
import jax
import jax.numpy as jnp
from jax import lax
from jax.sharding import PartitionSpec as P

TILE = 256
CAP = 2
exact_mode = lax.Precision.HIGHEST


def spread(shard, axis, root):
    mine = lax.axis_index(axis) == root
    return lax.psum(jnp.where(mine, shard, jnp.zeros_like(shard)), axis)


def padded_block(slot_data, slot_ids, block_index, tiles_per_block, tile_rows):
    local_tile = slot_ids - block_index * tiles_per_block
    pieces = []
    for tile_index in range(tiles_per_block):
        chosen = jnp.zeros((tile_rows, slot_data.shape[1]), slot_data.dtype)
        for member in range(slot_ids.shape[0]):
            chosen = jnp.where(
                local_tile[member] == tile_index,
                slot_data[member * tile_rows : (member + 1) * tile_rows],
                chosen,
            )
        pieces.append(chosen)
    return jnp.concatenate(pieces, axis=0)


def chosen_columns(inverse_block, slot_ids, block_index, tiles_per_block, tile_rows):
    local_tile = jnp.clip(slot_ids - block_index * tiles_per_block, 0, tiles_per_block - 1)
    pieces = [
        lax.dynamic_slice_in_dim(inverse_block, local_tile[member] * tile_rows, tile_rows, 1)
        for member in range(slot_ids.shape[0])
    ]
    return jnp.concatenate(pieces, axis=1)


def masked_rows(slot_data, slot_ids, tile_rows):
    live_rows = jnp.repeat(slot_ids >= 0, tile_rows)
    return jnp.where(live_rows[:, None], slot_data, jnp.zeros_like(slot_data))


def on_device(ancestor_inverse, factor_slots, slot_tiles, parent_factor, diag_inverse):
    row_count = lax.axis_size("row")
    col_count = lax.axis_size("col")
    row_index = lax.axis_index("row")
    col_index = lax.axis_index("col")
    block_rows, block_cols = ancestor_inverse.shape
    tile_rows = TILE
    tiles_per_block = block_cols // tile_rows
    node_count = factor_slots.shape[0]
    slot_count = CAP
    slot_rows = slot_count * tile_rows
    groups_per_row = col_count // row_count
    panel_rows = block_rows // col_count
    own_block = row_index * groups_per_row + col_index // row_count
    own_offset = col_index % row_count * panel_rows
    slot_start = col_index % groups_per_row * slot_rows
    owner_row = col_index // groups_per_row

    def finish(node, first_total, second_total, prev_diag):
        if node == 0:
            return (diag_inverse[0] - first_total, None)
        parent_link = parent_factor[node - 1].astype(jnp.float32)
        upper = -(second_total + jnp.dot(prev_diag, parent_link, precision=exact_mode))
        diagonal = (
            diag_inverse[node] - first_total - jnp.dot(parent_link.T, upper, precision=exact_mode)
        )
        return (diagonal, upper)

    def node_sums(node, first_part, second_part):
        if node == 0:
            return (lax.psum(first_part, ("row", "col")), None)
        return lax.psum((first_part, second_part), ("row", "col"))

    panels = []
    diagonals = []
    parents = []
    previous = None
    prev_diag = None
    for node in range(node_count):
        row_slots = lax.all_gather(factor_slots[node], "col", axis=0, tiled=True)
        mine = lax.dynamic_slice_in_dim(row_slots, slot_start, slot_rows, 0)
        col_slots = spread(mine, "row", owner_row)
        tiles_node = slot_tiles[node]
        col_ids = lax.dynamic_slice_in_dim(tiles_node, col_index * slot_count, slot_count)
        prepare_columns = chosen_columns(
            ancestor_inverse, col_ids, col_index, tiles_per_block, tile_rows
        )
        prepare_weights = masked_rows(col_slots, col_ids, tile_rows)
        own_ids = lax.dynamic_slice_in_dim(tiles_node, own_block * slot_count, slot_count)
        own_slots = lax.dynamic_slice_in_dim(
            row_slots, col_index // row_count * slot_rows, slot_rows, 0
        )
        own_padded = padded_block(own_slots, own_ids, own_block, tiles_per_block, tile_rows)
        own_rows = lax.dynamic_slice_in_dim(own_padded, own_offset, panel_rows, 0)
        row_padded = None
        columns, weights, own_rows, row_padded = (
            prepare_columns,
            prepare_weights,
            own_rows.astype(jnp.float32),
            row_padded,
        )
        second_part = None
        if node > 0:
            second_part = jnp.dot(previous.T, own_rows, precision=exact_mode)
        summed = lax.psum_scatter(
            jnp.dot(columns, weights, preferred_element_type=jnp.float32),
            "col",
            scatter_dimension=0,
            tiled=True,
        )
        column = -summed
        if node > 0:
            advance_parent_link = parent_factor[node - 1].astype(jnp.float32)
            column = column - jnp.dot(previous, advance_parent_link, precision=exact_mode)
        first_part = jnp.dot(own_rows.T, column, precision=exact_mode)
        first_total, second_total = node_sums(node, first_part, second_part)
        diagonal, upper = finish(node, first_total, second_total, prev_diag)
        panels.append(column.astype(jnp.bfloat16))
        diagonals.append(diagonal)
        if node > 0:
            parents.append(upper)
        previous = column
        prev_diag = diagonal
    return (jnp.stack(panels), jnp.stack(diagonals), jnp.stack(parents))


def solution(mesh):
    placed = (P("row", "col"), P(None, ("row", "col"), None), P(), P(), P())
    return jax.shard_map(
        on_device,
        mesh=mesh,
        in_specs=placed,
        out_specs=(P(None, ("row", "col"), None), P(), P()),
        check_vma=False,
    )
```

profile of v0, /device:TPU:8, one launch (start us, length us, event | category | flops | bytes accessed | tf_op | source)
XLA Modules:
  0.0 841.9 jit_solution(13287973406344088835)
XLA Ops:
  7.2 1.6 fusion.71
  8.9 0.7 all-gather.7.cloned.1.call-update
  9.6 0.7 all-gather.11.cloned.1.call-update
  10.4 51.9 %all-gather.9.cloned.1.call-done = bf16[1,2048,512]{2,1,0:T(8,128)(2,1)} async-done(((bf16[1,64,512]{2,1,0:T(8,128)(2,1)}), bf16[1,2048,512]{2,1,0:T(8,128)(2,1)}) %all-gather.9.cloned.1.call-update) | async-done | bytes 2097168 | tf_op jit(solution)/shard_map/all_gather | solution.py:84
  62.3 1.9 select_bitcast_fusion.1
  64.2 49.2 %all-gather.7.cloned.1.call-done = bf16[1,2048,512]{2,1,0:T(8,128)(2,1)} async-done(((bf16[1,64,512]{2,1,0:T(8,128)(2,1)}), bf16[1,2048,512]{2,1,0:T(8,128)(2,1)}) %all-gather.7.cloned.1.call-update) | async-done | bytes 2097168 | tf_op jit(solution)/shard_map/all_gather | solution.py:84
  113.4 1.9 select_bitcast_fusion.2
  115.3 49.2 %all-gather.11.cloned.1.call-done = bf16[1,2048,512]{2,1,0:T(8,128)(2,1)} async-done(((bf16[1,64,512]{2,1,0:T(8,128)(2,1)}), bf16[1,2048,512]{2,1,0:T(8,128)(2,1)}) %all-gather.11.cloned.1.call-update) | async-done | bytes 2097168 | tf_op jit(solution)/shard_map/all_gather | solution.py:84
  164.5 1.9 select_bitcast_fusion
  166.6 0.1 fusion.56
  166.6 0.6 fusion.75
  168.5 0.1 fusion.54
  168.6 0.6 fusion.77
  170.4 0.7 fusion.78
  172.4 0.1 compare_bitcast_fusion
  172.5 0.1 broadcast_in_dim.36
  172.6 6.8 constant_dynamic-slice_fusion.4
  179.5 66.0 %all-reduce.7.cloned.1.call-done = (bf16[512,512]{1,0:T(8,128)(2,1)}, bf16[512,512]{1,0:T(8,128)(2,1)}, bf16[512,512]{1,0:T(8,128)(2,1)}) async-done(((bf16[512,512]{1,0:T(8,128)(2,1)}, bf16[512,512]{1,0:T(8,128)(2,1)}, bf16[512,512]{1,0:T(8,128)(2,1)}), (bf16[512,512]{1,0:T(8,128)(2,1)}, bf16[512,512]{1,0:T(8,128)(2,1)}, bf16[512,512]{1,0:T(8,128)(2,1)})) %all-reduce.7.cloned.1.call-update) | async-done | bytes 1572880 | tf_op jit(solution)/shard_map/psum | solution.py:13
  245.4 6.5 fusion.4
  252.0 0.1 compare_bitcast_fusion.2
  252.2 6.5 fusion
  258.8 5.5 fusion.8
  264.4 0.2 all-reduce.5.cloned.1.call-start
  264.6 0.6 fusion.73
  272.8 0.6 fusion.74
  277.3 1.2 select_bitcast_fusion.8
  278.5 2.0 select_bitcast_fusion.10
  280.5 1.2 select_bitcast_fusion.5
  281.7 63.3 %reduce-scatter.6.cloned.1.call-done = f32[96,512]{1,0:T(8,128)} async-done(((f32[3072,512]{1,0:T(8,128)}), f32[96,512]{1,0:T(8,128)}) %reduce-scatter.6.cloned.1.call-update) | async-done | bytes 196624 | tf_op jit(solution)/shard_map/reduce_scatter | solution.py:109
  345.0 97.1 %reduce-scatter.4.cloned.1.call-done = f32[96,512]{1,0:T(8,128)} async-done(((f32[3072,512]{1,0:T(8,128)}), f32[96,512]{1,0:T(8,128)}) %reduce-scatter.4.cloned.1.call-update) | async-done | bytes 196624 | tf_op jit(solution)/shard_map/reduce_scatter | solution.py:109
  442.1 1.4 convolution_subtract_fusion.1
  443.5 1.7 fusion.69
  445.2 94.2 %reduce-scatter.8.cloned.1.call-done = f32[96,512]{1,0:T(8,128)} async-done(((f32[3072,512]{1,0:T(8,128)}), f32[96,512]{1,0:T(8,128)}) %reduce-scatter.8.cloned.1.call-update) | async-done | bytes 196624 | tf_op jit(solution)/shard_map/reduce_scatter | solution.py:109
  539.4 1.3 convolution_subtract_fusion
  540.7 1.7 fusion.67
  542.5 1.7 fusion.64
  544.2 1.7 fusion.39
  545.8 1.8 fusion.41
  547.8 0.7 pad_maximum_fusion.2
  548.5 274.5 %all-reduce.5.cloned.1.call-done = (f32[512,512]{1,0:T(8,128)}, f32[512,512]{1,0:T(8,128)}, f32[512,512]{1,0:T(8,128)}, f32[512,512]{1,0:T(8,128)}, f32[512,512]{1,0:T(8,128)}) async-done(((f32[512,512]{1,0:T(8,128)}, f32[512,512]{1,0:T(8,128)}, f32[512,512]{1,0:T(8,128)}, f32[512,512]{1,0:T(8,128)}, f32[512,512]{1,0:T(8,128)}), (f32[512,512]{1,0:T(8,128)}, f32[512,512]{1,0:T(8,128)}, f32[512,512]{1,0:T(8,128)}, ...) | async-done | bytes 5242896 | tf_op jit(solution)/shard_map/psum | solution.py:76
  823.1 1.9 fusion.29
  825.0 0.6 copy-done.1
  825.6 2.6 fusion.13
  828.2 1.1 fusion.16
  829.4 1.0 fusion.12
  830.4 1.1 fusion.15
  831.5 1.5 pad_maximum_fusion.1
  833.0 2.0 pad_maximum_fusion
  (39 shorter events, 0.8 us)
Async XLA Ops:
  7.2 159.4 %copy-start.8 = (s32[3,64]{1,0:T(4,128)S(1)}, s32[3,64]{1,0:T(4,128)}, u32[]{:S(2)}) copy-start(s32[3,64]{1,0:T(4,128)} %param.7) | copy-start | bytes 2308
  7.2 55.1 %all-gather.9.cloned.1.call-start = ((), (), s32[]{:S(2)}) async-start(), calls=%async_computation.7 | async-start | bytes 2162688 | tf_op jit(solution)/shard_map/all_gather | solution.py:84
  8.8 104.6 %all-gather.7.cloned.1.call-start = ((), (), s32[]{:S(2)}) async-start(), calls=%async_computation.6 | async-start | bytes 2162688 | tf_op jit(solution)/shard_map/all_gather | solution.py:84
  9.6 154.9 %all-gather.11.cloned.1.call-start = ((), (), s32[]{:S(2)}) async-start(), calls=%async_computation.8 | async-start | bytes 2162688 | tf_op jit(solution)/shard_map/all_gather | solution.py:84
  10.3 235.1 %all-reduce.7.cloned.1.call-start = ((), (), s32[]{:S(2)}) async-start(), calls=%async_computation.10 | async-start | bytes 3145728 | tf_op jit(solution)/shard_map/psum | solution.py:13
  166.5 178.5 %reduce-scatter.6.cloned.1.call-start = ((), (), s32[]{:S(2)}) async-start(), calls=%async_computation.4 | async-start | bytes 6488064 | tf_op jit(solution)/shard_map/reduce_scatter | solution.py:109
  252.0 190.1 %reduce-scatter.4.cloned.1.call-start = ((), (), s32[]{:S(2)}) async-start(), calls=%async_computation.3 | async-start | bytes 6488064 | tf_op jit(solution)/shard_map/reduce_scatter | solution.py:109
  258.7 280.7 %reduce-scatter.8.cloned.1.call-start = ((), (), s32[]{:S(2)}) async-start(), calls=%async_computation.5 | async-start | bytes 6488064 | tf_op jit(solution)/shard_map/reduce_scatter | solution.py:109
  264.4 177.7 %copy-start = (bf16[2,512,512]{2,1,0:T(8,128)(2,1)S(1)}, bf16[2,512,512]{2,1,0:T(8,128)(2,1)}, u32[]{:S(2)}) copy-start(bf16[2,512,512]{2,1,0:T(8,128)(2,1)} %param.8) | copy-start | bytes 3145732
  264.4 558.7 %all-reduce.5.cloned.1.call-start = ((), (), s32[]{:S(2)}) async-start(), calls=%async_computation.9 | async-start | bytes 10485760 | tf_op jit(solution)/shard_map/psum | solution.py:76
  443.5 100.7 %copy-start.2 = (f32[96,512]{1,0:T(8,128)S(1)}, f32[96,512]{1,0:T(8,128)}, u32[]{:S(2)}) copy-start(f32[96,512]{1,0:T(8,128)} %reduce-scatter.4.cloned.1.call-done) | copy-start | bytes 589828
  540.7 5.1 copy-start.4
  540.7 5.1 copy-start.5
  823.0 2.5 copy-start.1
  825.0 3.2 copy-start.7
  828.2 1.2 copy-start.3
  828.2 2.2 copy-start.6
Sparse Core Ops, SparseCore 0:
  11.1 51.0 all-gather.8
  65.4 47.9 all-gather.6
  116.5 47.9 all-gather.10
  167.0 78.4 all-reduce.6
  252.1 92.8 reduce-scatter.5
  348.9 93.1 reduce-scatter.3
  446.1 93.2 reduce-scatter.7
  547.8 275.1 all-reduce.4
where the time goes:
time: 843 us; the launch traced here: 842 us
  waiting for transfers between devices  747 us (89%)
  matrix products  35.6 us (4%)
  between operations  29.7 us (4%)
  other arithmetic  16.8 us (2%)
  local copies, waits for them, and re-layouts  12.5 us (1%)
    psum x1, waiting for transfers between devices, node_sums(): return lax.psum((first_part, second_part), ('row', 'col'))  275 us
    reduce_scatter x3, waiting for transfers between devices, on_device(): lax.psum_scatter(jnp.dot(columns, weights, preferred_element_type=jnp.flo...  255 us
    all_gather x3, waiting for transfers between devices, on_device(): row_slots = lax.all_gather(factor_slots[node], 'col', axis=0, tiled=True)  150 us
    psum x1, waiting for transfers between devices, spread(): return lax.psum(jnp.where(mine, shard, jnp.zeros_like(shard)), axis)  66 us
    dot_general x3, matrix products, on_device(): jnp.dot(columns, weights, preferred_element_type=jnp.float32)  18.5 us
  transfers between devices with their start and end apart: 8, of which 8 were waited for; matrix products, arithmetic and copies ran while one was open for 4% of the time, Pallas kernels for 0%

commit v1 on v0

--- a/solution.py
+++ b/solution.py
@@ -81,7 +81,10 @@
     previous = None
     prev_diag = None
     for node in range(node_count):
-        row_slots = lax.all_gather(factor_slots[node], "col", axis=0, tiled=True)
+        row_slots = jnp.concatenate(
+            lax.all_to_all(jnp.stack([factor_slots[node]] * lax.axis_size("col")), "col", 0, 0),
+            axis=0,
+        )
         mine = lax.dynamic_slice_in_dim(row_slots, slot_start, slot_rows, 0)
         col_slots = spread(mine, "row", owner_row)
         tiles_node = slot_tiles[node]

time: 843 us -> 788 us (0.935)
  waiting for transfers between devices: 747 us -> 616 us
  blocking collectives: 0 us -> 65.5 us
    all_gather x3 -> x0, waiting for transfers between devices: 150 us -> none  [on_device(): row_slots = lax.all_gather(factor_slots[node], 'col', axis=0, tiled=True)]
    all_to_all x0 -> x2, blocking collectives: none -> 65.5 us  [on_device(): lax.all_to_all(jnp.stack([factor_slots[node]] * lax.axis_size('col')), 'c...]
    all_to_all x0 -> x1, waiting for transfers between devices: none -> 22.7 us  [on_device(): lax.all_to_all(jnp.stack([factor_slots[node]] * lax.axis_size('col')), 'c...]
  transfers between devices with their start and end apart: 8 -> 6, of which waited for: 8 -> 6; matrix products, arithmetic and copies ran while one was open for 4% -> 5% of each run, Pallas kernels for 0% -> 0%
where the time goes in v1:
time: 788 us; the launch traced here: 787 us
  waiting for transfers between devices  616 us (78%)
  blocking collectives  65.5 us (8%)
  matrix products  36.2 us (5%)
  between operations  29.7 us (4%)
  local copies, waits for them, and re-layouts  16.3 us (2%)
  other arithmetic  16.3 us (2%)
    psum x1, waiting for transfers between devices, node_sums(): return lax.psum((first_part, second_part), ('row', 'col'))  275 us
    reduce_scatter x3, waiting for transfers between devices, on_device(): lax.psum_scatter(jnp.dot(columns, weights, preferred_element_type=jnp.flo...  251 us
    psum x1, waiting for transfers between devices, spread(): return lax.psum(jnp.where(mine, shard, jnp.zeros_like(shard)), axis)  66.9 us
    all_to_all x2, blocking collectives, on_device(): lax.all_to_all(jnp.stack([factor_slots[node]] * lax.axis_size('col')), 'c...  65.5 us
    all_to_all x1, waiting for transfers between devices, on_device(): lax.all_to_all(jnp.stack([factor_slots[node]] * lax.axis_size('col')), 'c...  22.7 us
    dot_general x3, matrix products, on_device(): jnp.dot(columns, weights, preferred_element_type=jnp.float32)  19.2 us
  transfers between devices with their start and end apart: 6, of which 6 were waited for; matrix products, arithmetic and copies ran while one was open for 5% of the time, Pallas kernels for 0%

profile of v1, /device:TPU:8, one launch (start us, length us, event | category | flops | bytes accessed | tf_op | source)
XLA Modules:
  0.0 787.3 jit_solution(2439904288077776930)
XLA Ops:
  7.2 0.9 slice_bitcast_fusion
  8.1 0.2 stack.46
  8.3 33.5 %all_to_all.15 = bf16[32,64,512]{2,1,0:T(8,128)(2,1)} all-to-all(bf16[32,64,512]{2,1,0:T(8,128)(2,1)S(1)} %stack.46), channel_id=1, replica_groups=mesh['row'=8,'col'=32] {'col'}, dimensions={0} | all-to-all | bytes 4194304 | tf_op jit(solution)/shard_map/all_to_all | solution.py:85
  41.8 0.2 stack.42
  42.1 32.0 %all_to_all.16 = bf16[32,64,512]{2,1,0:T(8,128)(2,1)} all-to-all(bf16[32,64,512]{2,1,0:T(8,128)(2,1)S(1)} %stack.42), channel_id=1, replica_groups=mesh['row'=8,'col'=32] {'col'}, dimensions={0} | all-to-all | bytes 4194304 | tf_op jit(solution)/shard_map/all_to_all | solution.py:85
  74.1 1.6 stack.44
  75.6 6.5 all-to-all-start.1
  82.2 1.9 dynamic-slice_select_fusion
  84.1 1.9 dynamic-slice_select_fusion.2
  86.0 22.7 %all-to-all-done.1 = bf16[32,64,512]{2,1,0:T(8,128)(2,1)S(1)} async-done(((bf16[32,64,512]{2,1,0:T(8,128)(2,1)}), bf16[32,64,512]{2,1,0:T(8,128)(2,1)S(1)}, u32[]{:S(2)}, u32[]{:S(2)}) %all-to-all-start.1) | async-done | bytes 2097184 | tf_op jit(solution)/shard_map/all_to_all | solution.py:85
  108.7 0.9 dynamic-slice_select_fusion.1
  109.8 0.6 fusion.74
  111.7 0.1 fusion.54
  111.7 0.6 fusion.76
  113.7 0.6 fusion.77
  115.7 7.7 constant_dynamic-slice_fusion.4
  123.5 66.9 %all-reduce.7.cloned.1.call-done = (bf16[512,512]{1,0:T(8,128)(2,1)}, bf16[512,512]{1,0:T(8,128)(2,1)}, bf16[512,512]{1,0:T(8,128)(2,1)}) async-done(((bf16[512,512]{1,0:T(8,128)(2,1)}, bf16[512,512]{1,0:T(8,128)(2,1)}, bf16[512,512]{1,0:T(8,128)(2,1)}), (bf16[512,512]{1,0:T(8,128)(2,1)}, bf16[512,512]{1,0:T(8,128)(2,1)}, bf16[512,512]{1,0:T(8,128)(2,1)})) %all-reduce.7.cloned.1.call-update) | async-done | bytes 1572880 | tf_op jit(solution)/shard_map/psum | solution.py:13
  190.4 6.5 fusion.4
  197.1 0.8 copy-done.14
  197.9 6.4 fusion
  204.5 0.9 copy-done.13
  205.3 6.3 fusion.8
  211.7 0.2 all-reduce.5.cloned.1.call-start
  212.0 0.6 fusion.72
  220.3 0.6 fusion.73
  224.8 2.0 select_select_fusion.2
  226.9 2.1 select_select_fusion.7
  228.9 1.0 select_select_fusion.5
  229.9 60.0 %reduce-scatter.6.cloned.1.call-done = f32[96,512]{1,0:T(8,128)} async-done(((f32[3072,512]{1,0:T(8,128)}), f32[96,512]{1,0:T(8,128)}) %reduce-scatter.6.cloned.1.call-update) | async-done | bytes 196624 | tf_op jit(solution)/shard_map/reduce_scatter | solution.py:112
  290.0 97.3 %reduce-scatter.4.cloned.1.call-done = f32[96,512]{1,0:T(8,128)} async-done(((f32[3072,512]{1,0:T(8,128)}), f32[96,512]{1,0:T(8,128)}) %reduce-scatter.4.cloned.1.call-update) | async-done | bytes 196624 | tf_op jit(solution)/shard_map/reduce_scatter | solution.py:112
  387.3 1.4 convolution_subtract_fusion.1
  388.7 1.6 fusion.69
  390.3 94.1 %reduce-scatter.8.cloned.1.call-done = f32[96,512]{1,0:T(8,128)} async-done(((f32[3072,512]{1,0:T(8,128)}), f32[96,512]{1,0:T(8,128)}) %reduce-scatter.8.cloned.1.call-update) | async-done | bytes 196624 | tf_op jit(solution)/shard_map/reduce_scatter | solution.py:112
  484.4 1.3 convolution_subtract_fusion
  485.7 1.7 fusion.67
  487.4 1.7 fusion.64
  489.2 1.7 fusion.39
  490.8 1.8 fusion.41
  492.8 0.7 pad_maximum_fusion.2
  493.5 275.3 %all-reduce.5.cloned.1.call-done = (f32[512,512]{1,0:T(8,128)}, f32[512,512]{1,0:T(8,128)}, f32[512,512]{1,0:T(8,128)}, f32[512,512]{1,0:T(8,128)}, f32[512,512]{1,0:T(8,128)}) async-done(((f32[512,512]{1,0:T(8,128)}, f32[512,512]{1,0:T(8,128)}, f32[512,512]{1,0:T(8,128)}, f32[512,512]{1,0:T(8,128)}, f32[512,512]{1,0:T(8,128)}), (f32[512,512]{1,0:T(8,128)}, f32[512,512]{1,0:T(8,128)}, f32[512,512]{1,0:T(8,128)}, ...) | async-done | bytes 5242896 | tf_op jit(solution)/shard_map/psum | solution.py:76
  768.8 1.9 fusion.29
  770.8 0.6 copy-done.1
  771.4 2.6 fusion.13
  774.0 1.1 fusion.16
  775.2 1.0 fusion.12
  776.2 1.1 fusion.15
  777.3 1.5 pad_maximum_fusion.1
  778.8 2.0 pad_maximum_fusion
  (49 shorter events, 1.0 us)
Async XLA Ops:
  75.6 33.1 %all-to-all-start.1 = ((bf16[32,64,512]{2,1,0:T(8,128)(2,1)}), bf16[32,64,512]{2,1,0:T(8,128)(2,1)S(1)}, u32[]{:S(2)}, u32[]{:S(2)}) async-start(bf16[32,64,512]{2,1,0:T(8,128)(2,1)} %stack.44), calls=%async_computation.2 | async-start | bytes 4194304 | tf_op jit(solution)/shard_map/all_to_all | solution.py:85
  82.1 27.6 %copy-start.12 = (s32[3,64]{1,0:T(4,128)S(1)}, s32[3,64]{1,0:T(4,128)}, u32[]{:S(2)}) copy-start(s32[3,64]{1,0:T(4,128)} %param.7) | copy-start | bytes 2308
  82.1 108.3 %all-reduce.7.cloned.1.call-start = ((), (), s32[]{:S(2)}) async-start(), calls=%async_computation.10 | async-start | bytes 3145728 | tf_op jit(solution)/shard_map/psum | solution.py:13
  109.6 180.4 %reduce-scatter.6.cloned.1.call-start = ((), (), s32[]{:S(2)}) async-start(), calls=%async_computation.7 | async-start | bytes 6488064 | tf_op jit(solution)/shard_map/reduce_scatter | solution.py:112
  196.9 1.0 copy-start.14
  196.9 190.4 %reduce-scatter.4.cloned.1.call-start = ((), (), s32[]{:S(2)}) async-start(), calls=%async_computation.6 | async-start | bytes 6488064 | tf_op jit(solution)/shard_map/reduce_scatter | solution.py:112
  204.3 1.0 copy-start.13
  204.3 280.1 %reduce-scatter.8.cloned.1.call-start = ((), (), s32[]{:S(2)}) async-start(), calls=%async_computation.8 | async-start | bytes 6488064 | tf_op jit(solution)/shard_map/reduce_scatter | solution.py:112
  211.7 175.5 %copy-start = (bf16[2,512,512]{2,1,0:T(8,128)(2,1)S(1)}, bf16[2,512,512]{2,1,0:T(8,128)(2,1)}, u32[]{:S(2)}) copy-start(bf16[2,512,512]{2,1,0:T(8,128)(2,1)} %param.8) | copy-start | bytes 3145732
  211.7 557.1 %all-reduce.5.cloned.1.call-start = ((), (), s32[]{:S(2)}) async-start(), calls=%async_computation.9 | async-start | bytes 10485760 | tf_op jit(solution)/shard_map/psum | solution.py:76
  229.9 257.5 %copy-start.3 = (bf16[256,512]{1,0:T(8,128)(2,1)S(1)}, bf16[256,512]{1,0:T(8,128)(2,1)}, u32[]{:S(2)}) copy-start(bf16[256,512]{1,0:T(8,128)(2,1)} %get-tuple-element.20) | copy-start | bytes 786436
  229.9 257.5 %copy-start.4 = (bf16[256,512]{1,0:T(8,128)(2,1)S(1)}, bf16[256,512]{1,0:T(8,128)(2,1)}, u32[]{:S(2)}) copy-start(bf16[256,512]{1,0:T(8,128)(2,1)} %get-tuple-element.21) | copy-start | bytes 786436
  229.9 257.5 %copy-start.5 = (bf16[256,512]{1,0:T(8,128)(2,1)S(1)}, bf16[256,512]{1,0:T(8,128)(2,1)}, u32[]{:S(2)}) copy-start(bf16[256,512]{1,0:T(8,128)(2,1)} %get-tuple-element.22) | copy-start | bytes 786436
  388.7 100.5 %copy-start.2 = (f32[96,512]{1,0:T(8,128)S(1)}, f32[96,512]{1,0:T(8,128)}, u32[]{:S(2)}) copy-start(f32[96,512]{1,0:T(8,128)} %reduce-scatter.4.cloned.1.call-done) | copy-start | bytes 589828
  485.7 5.1 copy-start.7
  485.7 5.1 copy-start.8
  485.7 5.1 copy-start.9
  768.8 2.5 copy-start.1
  770.7 3.2 copy-start.11
  773.9 1.2 copy-start.6
  774.0 2.2 copy-start.10
Sparse Core Ops, SparseCore 0:
  109.7 80.6 all-reduce.6
  197.0 92.8 reduce-scatter.5
  294.0 93.2 reduce-scatter.3
  391.1 93.2 reduce-scatter.7
  492.8 275.9 all-reduce.4
